TPU v7x, 256 devices: a whole 4x4x8 slice. The times are simulated.
256 devices in a mesh: dp: 64 (over z_lo, y, x, core), ckpt: 4 (over z_hi).
Axes of the slice: x: 4, y: 4, z: 8 (z_hi: 4, z_lo: 2; z = z_hi * 2 + z_lo), core: 2. Of those that a mesh axis runs over, the one named last changes fastest.
Arguments:
- layer_input: bfloat16 [32768, 6144], P(('dp', 'ckpt')), may hold values from -6 to 6
- out_grad: bfloat16 [32768, 6144], P(('dp', 'ckpt')), may hold values from -6 to 6
- router_weight: bfloat16 [32768], P(('dp', 'ckpt')), may hold values from 0.049804688 to 1
- token_slot: int32 [32768], P(('dp', 'ckpt')), may hold values from -1 to 7, as said below
- slot_token: int32 [2048], P(('dp', 'ckpt')), may hold values from -1 to 127, as said below
- gate_weight: bfloat16 [6144, 8192], P('ckpt', 'dp'), may hold values from -0.078125 to 0.078125
- up_weight: bfloat16 [6144, 8192], P('ckpt', 'dp'), may hold values from -0.078125 to 0.078125
- down_weight: bfloat16 [6144, 8192], P('ckpt', 'dp'), may hold values from -0.078125 to 0.078125
Outputs:
- input_grad: bfloat16 [32768, 6144], P(('dp', 'ckpt'))
- router_grad: float32 [32768], P(('dp', 'ckpt'))
- gate_grad: float32 [6144, 8192], P('ckpt', 'dp')
- up_grad: float32 [6144, 8192], P('ckpt', 'dp')
- down_grad: float32 [6144, 8192], P('ckpt', 'dp')
Inputs may be any that keep to these rules, and one draw needn't show every extreme that they name: `token_slot`: for each token, its row among the rows that its device sends to the expert, or -1 if the router did not send it there. A device's live rows are 0 to n - 1 for some n of 1 to 8. For each of a device's 8 rows, the index among that device's tokens of the token in it, or -1 for an empty row. Live rows come first; token_slot and slot_token are inverse to each other. In every draw all devices of some group along ckpt fill all 8 rows.
All inputs are finite; a program needn't handle non-finite values.
Results may differ from a plain program's by a relative error of at most 0.0049.
Values may be sent and summed in bfloat16 or wider, within the bound.
A program may use at most 128 MiB of HBM per device.

v0:
```python
import jax
import jax.numpy as jnp
from jax import lax
from jax.sharding import PartitionSpec as P


def local(
    layer_input,
    out_grad,
    router_weight,
    token_slot,
    slot_token,
    gate_weight,
    up_weight,
    down_weight,
):
    members = lax.axis_size("ckpt")
    row_count = slot_token.shape[0]
    is_live = slot_token >= 0
    safe_index = jnp.maximum(slot_token, 0)
    rows_input = jnp.where(
        is_live[:, None], jnp.take(layer_input, safe_index, axis=0), jnp.zeros((), jnp.bfloat16)
    )
    rows_grad = jnp.where(
        is_live[:, None], jnp.take(out_grad, safe_index, axis=0), jnp.zeros((), jnp.bfloat16)
    )
    rows_router = jnp.where(
        is_live, jnp.take(router_weight, safe_index, axis=0), jnp.zeros((), jnp.bfloat16)
    )
    router_tile = jnp.broadcast_to(rows_router[:, None], (row_count, members))
    quarter_input, quarter_grad, quarter_router = (
        lax.all_to_all(rows_input, "ckpt", split_axis=1, concat_axis=0, tiled=True),
        lax.all_to_all(rows_grad, "ckpt", split_axis=1, concat_axis=0, tiled=True),
        lax.all_to_all(router_tile, "ckpt", split_axis=1, concat_axis=0, tiled=True),
    )
    all_input, all_grad, all_router = (
        lax.all_gather(quarter_input, "dp", axis=0, tiled=True),
        lax.all_gather(quarter_grad, "dp", axis=0, tiled=True),
        lax.all_gather(quarter_router, "dp", axis=0, tiled=True),
    )
    gate_part = jnp.dot(all_input, gate_weight, preferred_element_type=jnp.float32)
    up_part = jnp.dot(all_input, up_weight, preferred_element_type=jnp.float32)
    back_part = jnp.dot(all_grad, down_weight, preferred_element_type=jnp.float32)
    gate_pre, up_pre, act_grad = lax.psum((gate_part, up_part, back_part), "ckpt")
    sigmoid_g = jax.nn.sigmoid(gate_pre)
    active = sigmoid_g * gate_pre * up_pre
    router_f = all_router.astype(jnp.float32)
    scaled = (router_f * active).astype(jnp.bfloat16)
    router_part = jnp.sum(active * act_grad, axis=1)
    act_delta = router_f * act_grad
    gate_delta = (act_delta * up_pre * sigmoid_g * (1.0 + gate_pre * (1.0 - sigmoid_g))).astype(
        jnp.bfloat16
    )
    up_delta = (act_delta * sigmoid_g * gate_pre).astype(jnp.bfloat16)
    input_part = jnp.einsum(
        "rh,dh->rd", gate_delta, gate_weight, preferred_element_type=jnp.float32
    )
    input_part = input_part + jnp.einsum(
        "rh,dh->rd", up_delta, up_weight, preferred_element_type=jnp.float32
    )
    input_sums, router_sums = (
        lax.psum_scatter(input_part, "dp", scatter_dimension=0, tiled=True),
        lax.psum_scatter(router_part, "dp", scatter_dimension=0, tiled=True),
    )
    input_quarters = input_sums.astype(jnp.bfloat16)
    input_rows = lax.all_to_all(input_quarters, "ckpt", split_axis=0, concat_axis=1, tiled=True)
    own_router = lax.dynamic_slice_in_dim(
        router_sums, lax.axis_index("ckpt") * row_count, row_count, 0
    )
    has_row = token_slot >= 0
    token_index = jnp.maximum(token_slot, 0)
    input_grad = jnp.where(
        has_row[:, None], jnp.take(input_rows, token_index, axis=0), jnp.zeros((), jnp.bfloat16)
    )
    router_grad = jnp.where(
        has_row, jnp.take(own_router, token_index, axis=0), jnp.zeros((), jnp.float32)
    )
    gate_grad = jnp.einsum("rd,rh->dh", all_input, gate_delta, preferred_element_type=jnp.float32)
    up_grad = jnp.einsum("rd,rh->dh", all_input, up_delta, preferred_element_type=jnp.float32)
    down_grad = jnp.einsum("rd,rh->dh", all_grad, scaled, preferred_element_type=jnp.float32)
    return (input_grad, router_grad, gate_grad, up_grad, down_grad)


def solution(mesh):
    return jax.shard_map(
        local,
        mesh=mesh,
        in_specs=(
            P(("dp", "ckpt"), None),
            P(("dp", "ckpt"), None),
            P(("dp", "ckpt")),
            P(("dp", "ckpt")),
            P(("dp", "ckpt")),
            P("ckpt", "dp"),
            P("ckpt", "dp"),
            P("ckpt", "dp"),
        ),
        out_specs=(
            P(("dp", "ckpt"), None),
            P(("dp", "ckpt")),
            P("ckpt", "dp"),
            P("ckpt", "dp"),
            P("ckpt", "dp"),
        ),
        check_vma=False,
    )
```

profile of v0, /device:TPU:32, one launch (start us, length us, event | category | flops | bytes accessed | tf_op | source)
XLA Modules:
  0.0 764.8 jit_solution(3806657502283674632)
XLA Ops:
  9.3 2.3 gather_fusion.2
  11.7 16.1 %all_to_all.73 = bf16[8,4,1536]{2,0,1:T(8,128)(2,1)} all-to-all(bf16[8,4,1536]{2,0,1:T(8,128)(2,1)S(1)} %bitcast.46), channel_id=1, replica_groups=mesh['dp'=64,'ckpt'=4] {'ckpt'}, dimensions={1} | all-to-all | bytes 196608 | tf_op jit(solution)/shard_map/all_to_all | solution.py:32
  27.9 11.5 %all_to_all.74 = bf16[8,4,1536]{2,0,1:T(8,128)(2,1)} all-to-all(bf16[8,4,1536]{2,0,1:T(8,128)(2,1)S(1)} %bitcast.45), channel_id=1, replica_groups=mesh['dp'=64,'ckpt'=4] {'ckpt'}, dimensions={1} | all-to-all | bytes 196608 | tf_op jit(solution)/shard_map/all_to_all | solution.py:33
  39.5 95.5 %all-gather.5.cloned.1.call-done = bf16[2048,1536]{1,0:T(8,128)(2,1)} async-done(((bf16[32,1536]{1,0:T(8,128)(2,1)}), bf16[2048,1536]{1,0:T(8,128)(2,1)}) %all-gather.5.cloned.1.call-update) | async-done | bytes 6291472 | tf_op jit(solution)/shard_map/all_gather | solution.py:37
  134.9 5.7 fusion.8
  140.7 2.8 fusion.7
  143.5 102.3 %all-gather.3.cloned.1.call-done = bf16[2048,1536]{1,0:T(8,128)(2,1)} async-done(((bf16[32,1536]{1,0:T(8,128)(2,1)}), bf16[2048,1536]{1,0:T(8,128)(2,1)}) %all-gather.3.cloned.1.call-update) | async-done | bytes 6291472 | tf_op jit(solution)/shard_map/all_gather | solution.py:38
  245.8 5.6 fusion.6
  252.7 6.4 all-to-all-start
  260.4 6.4 all-to-all-done
  267.1 153.7 %all-reduce = bf16[2048]{0:T(1024)(128)(2,1)S(1)} all-reduce(bf16[2048]{0:T(1024)(128)(2,1)S(1)} %dynamic-update-slice), channel_id=1, replica_groups=mesh['dp'=64,'ckpt'=4] {'dp'}, use_global_device_ids=true, to_apply=%add | all-reduce | flops 2048 | bytes 8192
  420.8 2.7 multiply_reduce_fusion
  423.6 1.8 fusion.9
  425.4 6.4 convolution_add_fusion
  432.5 141.2 %all-reduce.1 = f32[2048]{0:T(1024)S(1)} all-reduce(f32[2048]{0:T(1024)S(1)} %get-tuple-element.9), channel_id=3, replica_groups=mesh['dp'=64,'ckpt'=4] {'dp'}, use_global_device_ids=true, to_apply=%region_5.7.clone | all-reduce | flops 2048 | bytes 16384
  574.5 5.7 fusion.10
  580.2 5.7 fusion.11
  585.9 3.1 fusion
  589.0 149.7 %reduce-scatter.2.cloned.1.call-done = f32[32,1536]{1,0:T(8,128)} async-done(((f32[2048,1536]{1,0:T(8,128)}), f32[32,1536]{1,0:T(8,128)}) %reduce-scatter.2.cloned.1.call-update) | async-done | bytes 196624 | tf_op jit(solution)/shard_map/reduce_scatter | solution.py:62
  738.8 1.6 convert_bitcast_fusion
  740.3 6.4 all-to-all-start.3
  746.7 5.6 fusion.3
  752.3 3.1 all-to-all-done.3
  755.4 1.5 gather_fusion.1
  (56 shorter events, 6.7 us)
Async XLA Ops:
  7.2 1.5 copy-start
  7.2 127.7 %all-gather.5.cloned.1.call-start = ((), (), s32[]{:S(2)}) async-start(), calls=%async_computation.6 | async-start | bytes 6389760 | tf_op jit(solution)/shard_map/all_gather | solution.py:37
  8.7 132.0 %copy-start.4 = (bf16[1536,128]{1,0:T(8,128)(2,1)S(1)}, bf16[1536,128]{1,0:T(8,128)(2,1)}, u32[]{:S(2)}) copy-start(bf16[1536,128]{1,0:T(8,128)(2,1)} %param.16) | copy-start | bytes 1179652
  27.8 218.0 %all-gather.3.cloned.1.call-start = ((), (), s32[]{:S(2)}) async-start(), calls=%async_computation.5 | async-start | bytes 6389760 | tf_op jit(solution)/shard_map/all_gather | solution.py:38
  39.4 381.4 %all-reduce.5.cloned.1.call-start = ((), (), s32[]{:S(2)}) async-start(), calls=%async_computation.8 | async-start | bytes 6291456 | tf_op jit(solution)/shard_map/psum | solution.py:44
  134.9 5.7 copy-start.2
  140.7 105.2 %copy-start.7 = (bf16[1536,128]{1,0:T(8,128)(2,1)S(1)}, bf16[1536,128]{1,0:T(8,128)(2,1)}, u32[]{:S(2)}) copy-start(bf16[1536,128]{1,0:T(8,128)(2,1)} %param.17) | copy-start | bytes 1179652
  143.5 107.9 %copy-start.1 = (bf16[128]{0:T(256)(128)(2,1)S(1)}, bf16[128]{0:T(256)(128)(2,1)}, u32[]{:S(2)}) copy-start(bf16[128]{0:T(256)(128)(2,1)} %param.12) | copy-start | bytes 772
  143.5 108.5 %copy-start.10 = (s32[8]{0:T(128)S(1)}, s32[8]{0:T(128)}, u32[]{:S(2)}) copy-start(s32[8]{0:T(128)} %param.14) | copy-start | bytes 100
  143.5 115.6 %copy-start.8 = (u32[256]{0:T(256)S(1)}, u32[256]{0:T(256)}, u32[]{:S(2)}) copy-start(u32[256]{0:T(256)} %constant.88) | copy-start | bytes 3076
  251.4 172.2 %copy-start.3 = (bf16[1536,128]{1,0:T(8,128)(2,1)S(1)}, bf16[1536,128]{1,0:T(8,128)(2,1)}, u32[]{:S(2)}) copy-start(bf16[1536,128]{1,0:T(8,128)(2,1)} %param.15) | copy-start | bytes 1179652
  252.7 14.1 %all-to-all-start = ((bf16[8,4,1]{0,2,1:T(2,128)(2,1)}), bf16[8,4,1]{0,2,1:T(2,128)(2,1)S(1)}, u32[]{:S(2)}, u32[]{:S(2)}) async-start(bf16[8,4,1]{0,2,1:T(2,128)(2,1)} %broadcast_in_dim.80), calls=%async_computation | async-start | bytes 4096 | tf_op jit(solution)/shard_map/all_to_all | solution.py:34
  259.1 479.6 %reduce-scatter.2.cloned.1.call-start = ((), (), s32[]{:S(2)}) async-start(), calls=%async_computation.7 | async-start | bytes 12779520 | tf_op jit(solution)/shard_map/reduce_scatter | solution.py:62
  431.8 0.7 copy-start.9
  574.5 11.4 %slice-start = ((s8[6291456]{0:T(1024)(128)(4,1)}), s8[4194304]{0:T(1024)(128)(4,1)S(1)}, s32[]{:S(2)}) async-start(s8[6291456]{0:T(1024)(128)(4,1)} %bitcast.41), calls=%async_computation.9 | async-start | bytes 8388608
  574.5 11.4 %copy-start.5 = (f32[2048,128]{1,0:T(8,128)S(1)}, f32[2048,128]{1,0:T(8,128)}, u32[]{:S(2)}) copy-start(f32[2048,128]{1,0:T(8,128)} %get-tuple-element.6) | copy-start | bytes 3145732
  574.5 11.4 %copy-start.6 = (f32[2048,128]{1,0:T(8,128)S(1)}, f32[2048,128]{1,0:T(8,128)}, u32[]{:S(2)}) copy-start(f32[2048,128]{1,0:T(8,128)} %get-tuple-element.7) | copy-start | bytes 3145732
  580.2 5.7 slice-start.1
  740.3 15.1 %all-to-all-start.3 = ((bf16[4,8,1536]{2,1,0:T(8,128)(2,1)}), bf16[4,8,1536]{2,1,0:T(8,128)(2,1)S(1)}, u32[]{:S(2)}, u32[]{:S(2)}) async-start(bf16[4,8,1536]{2,1,0:T(8,128)(2,1)} %convert_bitcast_fusion), calls=%async_computation.4 | async-start | bytes 196608 | tf_op jit(solution)/shard_map/all_to_all | solution.py:66
Sparse Core Ops, SparseCore 0:
  27.9 106.9 all-gather.4
  136.8 108.9 all-gather.2
  251.5 131.6 all-reduce.4
  431.9 306.7 reduce-scatter.1
where the time goes:
time: 765 us
  waiting for transfers between devices  357 us (47%)
  blocking collectives  322 us (42%)
  matrix products  36.8 us (5%)
  between operations  15.2 us (2%)
  starting transfers between devices  12.9 us (2%)
  other arithmetic  12.8 us (2%)
    unnamed x2, blocking collectives  295 us
    reduce_scatter x1, waiting for transfers between devices, local(): lax.psum_scatter(input_part, 'dp', scatter_dimension=0, tiled=True)  150 us
    all_gather x1, waiting for transfers between devices, local(): lax.all_gather(quarter_grad, 'dp', axis=0, tiled=True)  102 us
    all_gather x1, waiting for transfers between devices, local(): lax.all_gather(quarter_input, 'dp', axis=0, tiled=True)  95.5 us
    all_to_all x1, blocking collectives, local(): lax.all_to_all(rows_input, 'ckpt', split_axis=1, concat_axis=0, tiled=True)  16.1 us
  transfers between devices with their start and end apart: 6, of which 5 were waited for; matrix products, arithmetic and copies ran while one was open for 4% of the time, Pallas kernels for 0%

commit v1 on v0

--- a/solution.py
+++ b/solution.py
@@ -34,7 +34,9 @@
         lax.all_to_all(router_tile, "ckpt", split_axis=1, concat_axis=0, tiled=True),
     )
     all_input, all_grad, all_router = (
-        lax.all_gather(quarter_input, "dp", axis=0, tiled=True),
+        jnp.concatenate(
+            lax.all_to_all(jnp.stack([quarter_input] * lax.axis_size("dp")), "dp", 0, 0), axis=0
+        ),
         lax.all_gather(quarter_grad, "dp", axis=0, tiled=True),
         lax.all_gather(quarter_router, "dp", axis=0, tiled=True),
     )

time: 765 us -> 736 us (0.962)
  waiting for transfers between devices: 357 us -> 314 us
    all_gather x1 -> x0, waiting for transfers between devices: 95.5 us -> none  [local(): lax.all_gather(quarter_input, 'dp', axis=0, tiled=True)]
    all_to_all x0 -> x1, waiting for transfers between devices: none -> 78.6 us  [local(): lax.all_to_all(jnp.stack([quarter_input] * lax.axis_size('dp')), 'dp', 0, 0)]
    all_gather x1, waiting for transfers between devices: 102 us -> 75.3 us  [local(): lax.all_gather(quarter_grad, 'dp', axis=0, tiled=True)]
    all_to_all x0 -> x1, starting transfers between devices: none -> 9.35 us  [local(): lax.all_to_all(jnp.stack([quarter_input] * lax.axis_size('dp')), 'dp', 0, 0)]
  transfers between devices with their start and end apart: 6 -> 6, of which waited for: 5 -> 5; matrix products, arithmetic and copies ran while one was open for 4% -> 5% of each run, Pallas kernels for 0% -> 0%
where the time goes in v1:
time: 736 us; the launch traced here: 735 us
  blocking collectives  323 us (44%)
  waiting for transfers between devices  314 us (43%)
  matrix products  39.4 us (5%)
  starting transfers between devices  19.8 us (3%)
  between operations  15.3 us (2%)
  other arithmetic  12.7 us (2%)
  local copies, waits for them, and re-layouts  10.8 us (1%)
    unnamed x2, blocking collectives  295 us
    reduce_scatter x1, waiting for transfers between devices, local(): lax.psum_scatter(input_part, 'dp', scatter_dimension=0, tiled=True)  150 us
    all_to_all x1, waiting for transfers between devices, local(): lax.all_to_all(jnp.stack([quarter_input] * lax.axis_size('dp')), 'dp', 0, 0)  78.6 us
    all_gather x1, waiting for transfers between devices, local(): lax.all_gather(quarter_grad, 'dp', axis=0, tiled=True)  75.3 us
    all_to_all x1, blocking collectives, local(): lax.all_to_all(rows_input, 'ckpt', split_axis=1, concat_axis=0, tiled=True)  16 us
  transfers between devices with their start and end apart: 6, of which 5 were waited for; matrix products, arithmetic and copies ran while one was open for 5% of the time, Pallas kernels for 0%

profile of v1, /device:TPU:32, one launch (start us, length us, event | category | flops | bytes accessed | tf_op | source)
XLA Modules:
  0.0 735.0 jit_solution(8124611549551368379)
XLA Ops:
  9.2 2.3 gather_fusion.2
  11.7 16.0 %all_to_all.75 = bf16[8,4,1536]{2,0,1:T(8,128)(2,1)S(1)} all-to-all(bf16[8,4,1536]{2,0,1:T(8,128)(2,1)S(1)} %bitcast.46), channel_id=1, replica_groups=mesh['dp'=64,'ckpt'=4] {'ckpt'}, dimensions={1} | all-to-all | bytes 196608 | tf_op jit(solution)/shard_map/all_to_all | solution.py:32
  27.6 11.5 %all_to_all.76 = bf16[8,4,1536]{2,0,1:T(8,128)(2,1)} all-to-all(bf16[8,4,1536]{2,0,1:T(8,128)(2,1)S(1)} %bitcast.45), channel_id=1, replica_groups=mesh['dp'=64,'ckpt'=4] {'ckpt'}, dimensions={1} | all-to-all | bytes 196608 | tf_op jit(solution)/shard_map/all_to_all | solution.py:33
  39.1 3.4 stack.5
  42.6 9.3 %all-to-all-start.3 = ((bf16[64,32,1536]{2,1,0:T(8,128)(2,1)}), bf16[64,32,1536]{2,1,0:T(8,128)(2,1)}, u32[]{:S(2)}, u32[]{:S(2)}) async-start(bf16[64,32,1536]{2,1,0:T(8,128)(2,1)} %stack.5), calls=%async_computation.3 | async-start | bytes 12582912 | tf_op jit(solution)/shard_map/all_to_all | solution.py:38
  52.7 78.6 %all-to-all-done.3 = bf16[64,32,1536]{2,1,0:T(8,128)(2,1)} async-done(((bf16[64,32,1536]{2,1,0:T(8,128)(2,1)}), bf16[64,32,1536]{2,1,0:T(8,128)(2,1)}, u32[]{:S(2)}, u32[]{:S(2)}) %all-to-all-start.3) | async-done | bytes 6291488 | tf_op jit(solution)/shard_map/all_to_all | solution.py:38
  131.3 5.5 fusion.8
  136.9 5.6 fusion.7
  142.5 75.3 %all-gather.2.cloned.1.call-done = bf16[2048,1536]{1,0:T(8,128)(2,1)} async-done(((bf16[32,1536]{1,0:T(8,128)(2,1)}), bf16[2048,1536]{1,0:T(8,128)(2,1)}) %all-gather.2.cloned.1.call-update) | async-done | bytes 6291472 | tf_op jit(solution)/shard_map/all_gather | solution.py:40
  217.8 5.5 fusion.6
  224.7 3.2 all-to-all-start
  229.2 6.3 all-to-all-done
  235.8 153.9 %all-reduce = bf16[2048]{0:T(1024)(128)(2,1)S(1)} all-reduce(bf16[2048]{0:T(1024)(128)(2,1)S(1)} %dynamic-update-slice), channel_id=1, replica_groups=mesh['dp'=64,'ckpt'=4] {'dp'}, use_global_device_ids=true, to_apply=%add | all-reduce | flops 2048 | bytes 8192
  389.7 2.7 multiply_reduce_fusion
  392.5 1.8 fusion.9
  394.3 6.4 convolution_add_fusion
  401.4 141.3 %all-reduce.1 = f32[2048]{0:T(1024)S(1)} all-reduce(f32[2048]{0:T(1024)S(1)} %get-tuple-element.9), channel_id=3, replica_groups=mesh['dp'=64,'ckpt'=4] {'dp'}, use_global_device_ids=true, to_apply=%region_5.7.clone | all-reduce | flops 2048 | bytes 16384
  543.4 5.7 fusion.10
  549.1 5.7 fusion.11
  554.8 3.1 fusion
  558.0 150.5 %reduce-scatter.2.cloned.1.call-done = f32[32,1536]{1,0:T(8,128)} async-done(((f32[2048,1536]{1,0:T(8,128)}), f32[32,1536]{1,0:T(8,128)}) %reduce-scatter.2.cloned.1.call-update) | async-done | bytes 196624 | tf_op jit(solution)/shard_map/reduce_scatter | solution.py:64
  710.0 7.1 all-to-all-start.4
  717.1 5.4 fusion.3
  722.5 3.0 all-to-all-done.4
  (54 shorter events, 10.4 us)
Async XLA Ops:
  7.2 1.5 copy-start
  42.6 88.8 %copy-start.2 = (bf16[1536,128]{1,0:T(8,128)(2,1)S(1)}, bf16[1536,128]{1,0:T(8,128)(2,1)}, u32[]{:S(2)}) copy-start(bf16[1536,128]{1,0:T(8,128)(2,1)} %param.15) | copy-start | bytes 1179652
  42.6 88.8 %all-to-all-start.3 = ((bf16[64,32,1536]{2,1,0:T(8,128)(2,1)}), bf16[64,32,1536]{2,1,0:T(8,128)(2,1)}, u32[]{:S(2)}, u32[]{:S(2)}) async-start(bf16[64,32,1536]{2,1,0:T(8,128)(2,1)} %stack.5), calls=%async_computation.3 | async-start | bytes 12582912 | tf_op jit(solution)/shard_map/all_to_all | solution.py:38
  51.9 85.0 %copy-start.3 = (bf16[1536,128]{1,0:T(8,128)(2,1)S(1)}, bf16[1536,128]{1,0:T(8,128)(2,1)}, u32[]{:S(2)}) copy-start(bf16[1536,128]{1,0:T(8,128)(2,1)} %param.16) | copy-start | bytes 1179652
  51.9 165.9 %all-gather.2.cloned.1.call-start = ((), (), s32[]{:S(2)}) async-start(), calls=%async_computation.6 | async-start | bytes 6389760 | tf_op jit(solution)/shard_map/all_gather | solution.py:40
  52.7 337.1 %all-reduce.5.cloned.1.call-start = ((), (), s32[]{:S(2)}) async-start(), calls=%async_computation.8 | async-start | bytes 6291456 | tf_op jit(solution)/shard_map/psum | solution.py:46
  136.9 80.9 %copy-start.6 = (bf16[1536,128]{1,0:T(8,128)(2,1)S(1)}, bf16[1536,128]{1,0:T(8,128)(2,1)}, u32[]{:S(2)}) copy-start(bf16[1536,128]{1,0:T(8,128)(2,1)} %param.17) | copy-start | bytes 1179652
  142.5 80.9 %copy-start.1 = (bf16[128]{0:T(256)(128)(2,1)S(1)}, bf16[128]{0:T(256)(128)(2,1)}, u32[]{:S(2)}) copy-start(bf16[128]{0:T(256)(128)(2,1)} %param.12) | copy-start | bytes 772
  142.5 81.5 %copy-start.9 = (s32[8]{0:T(128)S(1)}, s32[8]{0:T(128)}, u32[]{:S(2)}) copy-start(s32[8]{0:T(128)} %param.14) | copy-start | bytes 100
  142.5 85.4 %copy-start.7 = (u32[256]{0:T(256)S(1)}, u32[256]{0:T(256)}, u32[]{:S(2)}) copy-start(u32[256]{0:T(256)} %constant.88) | copy-start | bytes 3076
  224.7 10.9 %all-to-all-start = ((bf16[8,4,1]{0,2,1:T(2,128)(2,1)}), bf16[8,4,1]{0,2,1:T(2,128)(2,1)S(1)}, u32[]{:S(2)}, u32[]{:S(2)}) async-start(bf16[8,4,1]{0,2,1:T(2,128)(2,1)} %broadcast_in_dim.80), calls=%async_computation | async-start | bytes 4096 | tf_op jit(solution)/shard_map/all_to_all | solution.py:34
  227.9 480.5 %reduce-scatter.2.cloned.1.call-start = ((), (), s32[]{:S(2)}) async-start(), calls=%async_computation.7 | async-start | bytes 12779520 | tf_op jit(solution)/shard_map/reduce_scatter | solution.py:64
  400.7 0.7 copy-start.8
  543.4 11.4 %slice-start = ((s8[6291456]{0:T(1024)(128)(4,1)}), s8[4194304]{0:T(1024)(128)(4,1)S(1)}, s32[]{:S(2)}) async-start(s8[6291456]{0:T(1024)(128)(4,1)} %bitcast.42), calls=%async_computation.9 | async-start | bytes 8388608
  543.4 11.4 %copy-start.4 = (f32[2048,128]{1,0:T(8,128)S(1)}, f32[2048,128]{1,0:T(8,128)}, u32[]{:S(2)}) copy-start(f32[2048,128]{1,0:T(8,128)} %get-tuple-element.6) | copy-start | bytes 3145732
  543.4 11.4 %copy-start.5 = (f32[2048,128]{1,0:T(8,128)S(1)}, f32[2048,128]{1,0:T(8,128)}, u32[]{:S(2)}) copy-start(f32[2048,128]{1,0:T(8,128)} %get-tuple-element.7) | copy-start | bytes 3145732
  549.1 5.7 slice-start.1
  710.0 15.6 %all-to-all-start.4 = ((bf16[4,8,1536]{2,1,0:T(8,128)(2,1)}), bf16[4,8,1536]{2,1,0:T(8,128)(2,1)S(1)}, u32[]{:S(2)}, u32[]{:S(2)}) async-start(bf16[4,8,1536]{2,1,0:T(8,128)(2,1)} %convert_bitcast_fusion), calls=%async_computation.5 | async-start | bytes 196608 | tf_op jit(solution)/shard_map/all_to_all | solution.py:68
Sparse Core Ops, SparseCore 0:
  54.6 163.1 all-gather.1
  223.5 128.7 all-reduce.4
  400.8 307.5 reduce-scatter.1
